TPU v7x, 32 devices: a whole 2x2x4 slice. The times are simulated.
32 devices in a mesh: coord: 8 (over z, y), cohort: 4 (over x, core).
Axes of the slice: x: 2, y: 2, z: 4, core: 2. Of those that a mesh axis runs over, the one named last changes fastest.
Arguments:
- shapes: bfloat16 [4, 1024, 32768], P('cohort', None, 'coord'), may hold values from -6 to 6
- sketch_signs: int32 [4, 1024, 128], P('cohort'), may hold values from -1 to 1
- merge_sketch: float32 [2, 2, 128, 128], replicated, may hold values from -1.5 to 1.5
Outputs:
- basis: float32 [4, 32768, 128], P('cohort', 'coord')
- scores: float32 [4, 1024, 128], P('cohort', 'coord')
All inputs are finite; a program needn't handle non-finite values.
Results may differ from a plain program's by a relative error of at most 0.0086.
Values sent between devices are 32-bit elements; how exact they have to be, the bound alone decides.
A program may use at most 64 MiB of HBM per device.

v0:
```python
import math
import jax
import jax.numpy as jnp
from jax import lax
from jax.sharding import PartitionSpec as P

LEVELS = 2


def from_partner(shard, axis, distance):
    return lax.ppermute(shard, axis, [(i, i ^ 1 << distance) for i in range(lax.axis_size(axis))])


def lower_inverse(gram):
    factor = jnp.linalg.cholesky(gram)
    ident = jnp.eye(gram.shape[0], dtype=gram.dtype)
    inverse = jax.scipy.linalg.solve_triangular(factor, ident, lower=True)
    return inverse.T


def inverse_all(gram):
    return lower_inverse(gram)


def orthonormal(mixed):
    gram = jnp.einsum("...pk,...pl->...kl", mixed, mixed, precision=lax.Precision.HIGHEST)
    gram = lax.psum(gram, "coord")
    return jnp.matmul(mixed, inverse_all(gram), precision=lax.Precision.HIGHEST)


def on_device(shapes, sketch_signs, merge_sketch):
    data = shapes[0].astype(jnp.float32)
    centered = (data - jnp.mean(data, axis=0, keepdims=True)).astype(jnp.bfloat16)
    signs = sketch_signs[0].astype(jnp.bfloat16)
    sketch = lax.dot_general(
        centered, signs, (((0,), (0,)), ((), ())), preferred_element_type=jnp.float32
    )
    current = orthonormal(sketch)
    position = lax.axis_index("cohort")
    for level in range(LEVELS):
        partner = from_partner(current, "cohort", level)
        upper_side = position >> level & 1 == 1
        lower_basis = jnp.where(upper_side, partner, current)
        upper_basis = jnp.where(upper_side, current, partner)
        mixed = jnp.matmul(lower_basis, merge_sketch[level, 0], precision=lax.Precision.HIGHEST)
        mixed = mixed + jnp.matmul(
            upper_basis, merge_sketch[level, 1], precision=lax.Precision.HIGHEST
        )
        current = orthonormal(mixed)
    width = current.shape[1]
    total_coords = current.shape[0] * lax.axis_size("coord")
    rounded = current.astype(jnp.bfloat16)
    sums = lax.psum_scatter(
        jnp.dot(centered, rounded, preferred_element_type=jnp.float32),
        "coord",
        scatter_dimension=0,
        tiled=True,
    )
    factor = 4.0 * math.sqrt(width / total_coords)
    basis_out = current * math.sqrt(total_coords)
    return (basis_out[None], (sums * factor)[None])


def solution(mesh):
    placed = (P("cohort", None, "coord"), P("cohort", None, None), P())
    return jax.shard_map(
        on_device,
        mesh=mesh,
        in_specs=placed,
        out_specs=(P("cohort", "coord", None), P("cohort", "coord", None)),
        check_vma=False,
    )
```

profile of v0, /device:TPU:0, one launch (start us, length us, event | category | flops | bytes accessed | tf_op | source)
XLA Modules:
  0.0 468.8 jit_solution(535079962595938200)
XLA Ops:
  7.2 4.7 %convert_reduce_fusion = f32[4096]{0:T(1024)S(1)} fusion(bf16[1,1024,4096]{2,1,0:T(8,128)(2,1)} %param.6), kind=kLoop, calls=%fused_computation.2 | loop fusion | flops 8384512 | bytes 8404992 | tf_op jit(solution)/shard_map/reduce_sum | solution.py:33
  13.0 3.8 fusion.6
  16.8 4.1 fusion.46
  21.4 71.6 %all-reduce.4.cloned.1.call-done = f32[128,128]{0,1:T(8,128)} async-done(((f32[128,128]{0,1:T(8,128)}), f32[128,128]{0,1:T(8,128)}) %all-reduce.4.cloned.1.call-update) | async-done | bytes 65552 | tf_op jit(solution)/shard_map/psum | solution.py:27
  94.8 11.7 %cholesky.59 = f32[128,128]{1,0:T(8,128)S(1)} custom-call(f32[128,128]{1,0:T(8,128)S(1)} %fusion.41), custom_call_target="Cholesky" | custom-call | tf_op jit(solution)/shard_map/jit(cholesky)/cholesky | solution.py:15
  107.9 9.8 %custom-call.7 = f32[1,128,128]{1,2,0:T(8,128)S(1)} custom-call(f32[1,128,128]{2,1,0:T(8,128)S(1)} %fusion.29), custom_call_target="InvertDiagBlocksLowerTriangular" | custom-call | tf_op jit(solution)/shard_map/jit(_solve_triangular)/triangular_solve | solution.py:17
  118.0 3.1 fusion.47
  121.1 4.4 collective-permute-done
  128.7 3.4 convolution_add_fusion.1
  132.2 4.1 fusion.48
  136.3 70.6 %all-reduce.6.cloned.1.call-done = f32[128,128]{0,1:T(8,128)} async-done(((f32[128,128]{0,1:T(8,128)}), f32[128,128]{0,1:T(8,128)}) %all-reduce.6.cloned.1.call-update) | async-done | bytes 65552 | tf_op jit(solution)/shard_map/psum | solution.py:27
  208.8 11.7 %cholesky.70 = f32[128,128]{1,0:T(8,128)S(1)} custom-call(f32[128,128]{1,0:T(8,128)S(1)} %fusion.37), custom_call_target="Cholesky" | custom-call | tf_op jit(solution)/shard_map/jit(cholesky)/cholesky | solution.py:15
  221.8 9.8 %custom-call.8 = f32[1,128,128]{1,2,0:T(8,128)S(1)} custom-call(f32[1,128,128]{2,1,0:T(8,128)S(1)} %fusion.30), custom_call_target="InvertDiagBlocksLowerTriangular" | custom-call | tf_op jit(solution)/shard_map/jit(_solve_triangular)/triangular_solve | solution.py:17
  231.9 3.1 fusion.49
  236.5 44.3 %collective-permute-done.1 = f32[4096,128]{1,0:T(8,128)S(1)} collective-permute-done((f32[4096,128]{1,0:T(8,128)}, f32[4096,128]{1,0:T(8,128)S(1)}, u32[]{:S(2)}, u32[]{:S(2)}) %collective-permute-start.1) | collective-permute-done | bytes 2097184 | tf_op jit(solution)/shard_map/ppermute | solution.py:11
  284.0 3.5 convolution_add_fusion
  287.5 4.1 fusion.50
  291.6 70.8 %all-reduce.8.cloned.1.call-done = f32[128,128]{0,1:T(8,128)} async-done(((f32[128,128]{0,1:T(8,128)}), f32[128,128]{0,1:T(8,128)}) %all-reduce.8.cloned.1.call-update) | async-done | bytes 65552 | tf_op jit(solution)/shard_map/psum | solution.py:27
  364.3 11.7 %cholesky.81 = f32[128,128]{1,0:T(8,128)S(1)} custom-call(f32[128,128]{1,0:T(8,128)S(1)} %fusion.33), custom_call_target="Cholesky" | custom-call | tf_op jit(solution)/shard_map/jit(cholesky)/cholesky | solution.py:15
  377.3 9.8 %custom-call.9 = f32[1,128,128]{1,2,0:T(8,128)S(1)} custom-call(f32[1,128,128]{2,1,0:T(8,128)S(1)} %fusion.31), custom_call_target="InvertDiagBlocksLowerTriangular" | custom-call | tf_op jit(solution)/shard_map/jit(_solve_triangular)/triangular_solve | solution.py:17
  387.4 1.9 fusion.51
  390.7 6.5 %fusion.3 = f32[1024,128]{1,0:T(8,128)} fusion(bf16[1,1024,4096]{2,1,0:T(8,128)(2,1)} %param.6, f32[4096]{0:T(1024)S(1)} %broadcast_multiply_fusion, f32[4096,128]{1,0:T(8,128)S(1)} %fusion.51), kind=kOutput, calls=%fused_computation.6 | convolution fusion | flops 1086849024 | bytes 11026432 | tf_op jit(solution)/shard_map/dot_general | solution.py:54
  397.2 3.1 multiply_bitcast_fusion
  400.3 60.1 %reduce-scatter.2.cloned.1.call-done = f32[128,128]{1,0:T(8,128)} async-done(((f32[1024,128]{1,0:T(8,128)}), f32[128,128]{1,0:T(8,128)}) %reduce-scatter.2.cloned.1.call-update) | async-done | bytes 65552 | tf_op jit(solution)/shard_map/reduce_scatter | solution.py:53
  (42 shorter events, 22.6 us)
Async XLA Ops:
  7.2 85.9 %all-reduce.4.cloned.1.call-start = ((), (), s32[]{:S(2)}) async-start(), calls=%async_computation.1 | async-start | bytes 131072 | tf_op jit(solution)/shard_map/psum | solution.py:27
  7.2 5.8 %copy-start = (bf16[1,1024,4096]{2,1,0:T(8,128)(2,1)S(1)}, bf16[1,1024,4096]{2,1,0:T(8,128)(2,1)}, u32[]{:S(2)}) copy-start(bf16[1,1024,4096]{2,1,0:T(8,128)(2,1)} %param.6) | copy-start | bytes 25165828
  20.9 186.1 %all-reduce.6.cloned.1.call-start = ((), (), s32[]{:S(2)}) async-start(), calls=%async_computation.2 | async-start | bytes 131072 | tf_op jit(solution)/shard_map/psum | solution.py:27
  118.0 8.9 %copy-start.4 = (f32[2,2,128,128]{3,2,1,0:T(8,128)S(1)}, f32[2,2,128,128]{3,2,1,0:T(8,128)}, u32[]{:S(2)}) copy-start(f32[2,2,128,128]{3,2,1,0:T(8,128)} %param.8) | copy-start | bytes 786436
  121.1 4.4 collective-permute-start
  125.5 1.4 copy-start.1
  136.3 226.2 %all-reduce.8.cloned.1.call-start = ((), (), s32[]{:S(2)}) async-start(), calls=%async_computation.3 | async-start | bytes 131072 | tf_op jit(solution)/shard_map/psum | solution.py:27
  235.0 45.7 %collective-permute-start.1 = (f32[4096,128]{1,0:T(8,128)}, f32[4096,128]{1,0:T(8,128)S(1)}, u32[]{:S(2)}, u32[]{:S(2)}) collective-permute-start(f32[4096,128]{1,0:T(8,128)} %fusion.49), channel_id=1, source_target_pairs={{0,2},{1,3},{2,0},{3,1},{4,6},{5,7},{6,4},{7,5},{8,10},{9,11},{10,... | collective-permute-start | bytes 6291464 | tf_op jit(solution)/shard_map/ppermute | solution.py:11
  280.8 1.4 copy-start.2
  291.6 168.8 %reduce-scatter.2.cloned.1.call-start = ((), (), s32[]{:S(2)}) async-start(), calls=%async_computation.4 | async-start | bytes 589824 | tf_op jit(solution)/shard_map/reduce_scatter | solution.py:53
  389.3 1.3 copy-start.3
Sparse Core Ops, SparseCore 0:
  21.0 71.9 all-reduce.3
  136.4 70.5 all-reduce.5
  291.7 70.7 all-reduce.7
  397.3 63.0 reduce-scatter.1
where the time goes:
time: 475 us; the launch traced here: 469 us
  waiting for transfers between devices  322 us (68%)
  other arithmetic  80.4 us (17%)
  matrix products  42.3 us (9%)
  between operations  14.3 us (3%)
  local copies, waits for them, and re-layouts  7.82 us (2%)
    psum x3, waiting for transfers between devices, orthonormal(): gram = lax.psum(gram, 'coord')  213 us
    reduce_scatter x1, waiting for transfers between devices, on_device(): lax.psum_scatter(jnp.dot(centered, rounded, preferred_element_type=jnp.fl...  60.1 us
    ppermute x2, waiting for transfers between devices, from_partner(): lax.ppermute(shard, axis, [(i, i ^ 1 << distance) for i in range(lax.axis...  48.6 us
    another operation x9, other arithmetic, lower_inverse(): factor = jnp.linalg.cholesky(gram)  37.2 us
    another operation x6, other arithmetic, lower_inverse(): inverse = jax.scipy.linalg.solve_triangular(factor, ident, lower=True)  31.4 us
    dot_general x3, matrix products, orthonormal(): jnp.einsum('...pk,...pl->...kl', mixed, mixed, precision=lax.Precision.HI...  12.3 us
  transfers between devices with their start and end apart: 6, of which 6 were waited for; matrix products, arithmetic and copies ran while one was open for 1% of the time, Pallas kernels for 0%

commit v1 on v0

--- a/solution.py
+++ b/solution.py
@@ -5,6 +5,11 @@
 from jax.sharding import PartitionSpec as P
 
 LEVELS = 2
+
+
+def part_stages_all(my_data):
+    all_rows = lax.all_gather(my_data, axis_name="coord")
+    return jnp.sum(all_rows, 0)
 
 
 def from_partner(shard, axis, distance):
@@ -24,7 +29,7 @@
 
 def orthonormal(mixed):
     gram = jnp.einsum("...pk,...pl->...kl", mixed, mixed, precision=lax.Precision.HIGHEST)
-    gram = lax.psum(gram, "coord")
+    gram = part_stages_all(gram)
     return jnp.matmul(mixed, inverse_all(gram), precision=lax.Precision.HIGHEST)
 
 

time: 475 us -> 349 us (0.73)
  waiting for transfers between devices: 322 us -> 106 us
  blocking collectives: 0 us -> 96.1 us
    psum x3 -> x0, waiting for transfers between devices: 213 us -> none  [orthonormal(): gram = lax.psum(gram, 'coord')]
    all_gather x0 -> x3, blocking collectives: none -> 96.1 us  [part_stages_all(): all_rows = lax.all_gather(my_data, axis_name='coord')]
    ppermute x2, waiting for transfers between devices: 48.6 us -> 43.2 us  [from_partner(): lax.ppermute(shard, axis, [(i, i ^ 1 << distance) for i in range(lax.axis...]
  transfers between devices with their start and end apart: 6 -> 3, of which waited for: 6 -> 3; matrix products, arithmetic and copies ran while one was open for 1% -> 1% of each run, Pallas kernels for 0% -> 0%
where the time goes in v1:
time: 349 us; the launch traced here: 343 us
  waiting for transfers between devices  106 us (30%)
  blocking collectives  96.1 us (28%)
  other arithmetic  78 us (22%)
  matrix products  42.4 us (12%)
  between operations  14.7 us (4%)
  local copies, waits for them, and re-layouts  3.97 us (1%)
    all_gather x3, blocking collectives, part_stages_all(): all_rows = lax.all_gather(my_data, axis_name='coord')  96.1 us
    reduce_scatter x1, waiting for transfers between devices, on_device(): lax.psum_scatter(jnp.dot(centered, rounded, preferred_element_type=jnp.fl...  63 us
    ppermute x2, waiting for transfers between devices, from_partner(): lax.ppermute(shard, axis, [(i, i ^ 1 << distance) for i in range(lax.axis...  43.2 us
    another operation x9, other arithmetic, lower_inverse(): factor = jnp.linalg.cholesky(gram)  37.2 us
    another operation x6, other arithmetic, lower_inverse(): inverse = jax.scipy.linalg.solve_triangular(factor, ident, lower=True)  31.4 us
    dot_general x3, matrix products, orthonormal(): jnp.einsum('...pk,...pl->...kl', mixed, mixed, precision=lax.Precision.HI...  10.5 us
    dot_general x3, matrix products, orthonormal(): return jnp.matmul(mixed, inverse_all(gram), precision=lax.Precision.HIGHEST)  8.47 us
  transfers between devices with their start and end apart: 3, of which 3 were waited for; matrix products, arithmetic and copies ran while one was open for 1% of the time, Pallas kernels for 0%

profile of v1, /device:TPU:0, one launch (start us, length us, event | category | flops | bytes accessed | tf_op | source)
XLA Modules:
  0.0 343.0 jit_solution(11687555814793687419)
XLA Ops:
  7.2 4.7 %convert_reduce_fusion = f32[4096]{0:T(1024)S(1)} fusion(bf16[1,1024,4096]{2,1,0:T(8,128)(2,1)} %param.6), kind=kLoop, calls=%fused_computation.2 | loop fusion | flops 8384512 | bytes 8404992 | tf_op jit(solution)/shard_map/reduce_sum | solution.py:38
  13.0 3.8 %fusion.6 = f32[4096,128]{1,0:T(8,128)S(1)} fusion(bf16[1,1024,4096]{2,1,0:T(8,128)(2,1)S(1)} %copy-done.2, f32[4096]{0:T(1024)S(1)} %broadcast_multiply_fusion, s32[1,1024,128]{2,1,0:T(8,128)} %param.7), kind=kOutput, calls=%fused_computation.8 | convolution fusion | flops 1086455808 | bytes 11026432 | tf_op jit(solution)/shard_map/dot_general | solution.py:40
  16.8 3.6 %fusion.46 = f32[128,128]{1,0:T(8,128)S(1)} fusion(f32[4096,128]{1,0:T(8,128)S(1)} %fusion.6), kind=kOutput, calls=%fused_computation.66 | convolution fusion | flops 805306368 | bytes 2162688 | tf_op jit(solution)/shard_map/...pk,...pl->...kl/dot_general | solution.py:31
  20.4 33.5 %all-gather = f32[1024,128]{1,0:T(8,128)S(1)} all-gather(f32[128,128]{1,0:T(8,128)S(1)} %fusion.46), channel_id=2, replica_groups=mesh['coord'=8,'cohort'=4] {'coord'}, dimensions={0}, use_global_device_ids=true | all-gather | bytes 589824 | tf_op jit(solution)/shard_map/all_gather | solution.py:11
  54.1 11.7 %cholesky.59 = f32[128,128]{1,0:T(8,128)S(1)} custom-call(f32[128,128]{1,0:T(8,128)S(1)} %fusion.41), custom_call_target="Cholesky" | custom-call | tf_op jit(solution)/shard_map/jit(cholesky)/cholesky | solution.py:20
  67.1 9.8 %custom-call.7 = f32[1,128,128]{1,2,0:T(8,128)S(1)} custom-call(f32[1,128,128]{2,1,0:T(8,128)S(1)} %fusion.29), custom_call_target="InvertDiagBlocksLowerTriangular" | custom-call | tf_op jit(solution)/shard_map/jit(_solve_triangular)/triangular_solve | solution.py:22
  77.3 3.4 %fusion.47 = f32[4096,128]{1,0:T(8,128)S(1)} fusion(f32[4096,128]{1,0:T(8,128)} %copy-done.1, f32[128,128]{1,0:T(8,128)S(1)} %fusion.27), kind=kOutput, calls=%fused_computation.67 | convolution fusion | flops 805306368 | bytes 4259840 | tf_op jit(solution)/shard_map/dot_general | solution.py:33
  80.8 4.3 %collective-permute-done = f32[4096,128]{1,0:T(8,128)} collective-permute-done((f32[4096,128]{1,0:T(8,128)S(1)}, f32[4096,128]{1,0:T(8,128)}, u32[]{:S(2)}, u32[]{:S(2)}) %collective-permute-start) | collective-permute-done | bytes 2097184 | tf_op jit(solution)/shard_map/ppermute | solution.py:16
  85.1 3.5 %fusion.13 = f32[4096,128]{1,0:T(8,128)S(1)} fusion(f32[4096,128]{1,0:T(8,128)S(1)} %fusion.47, f32[4096,128]{1,0:T(8,128)} %collective-permute-done, pred[]{:T(512)S(6)} %eq.16, f32[2,2,128,128]{3,2,1,0:T(8,128)S(1)} %copy-done.5), kind=kOutput, calls=%fused_computation.17 | convolution fusion | flops 805830656 | bytes 6356993 | tf_op jit(solution)/shard_map/dot_general | solution.py:51
  88.5 3.4 %convolution_add_fusion.1 = f32[4096,128]{1,0:T(8,128)S(1)} fusion(f32[4096,128]{1,0:T(8,128)S(1)} %fusion.13, f32[4096,128]{1,0:T(8,128)} %collective-permute-done, f32[4096,128]{1,0:T(8,128)} %copy-done, pred[]{:T(512)S(6)} %eq.16, f32[2,2,128,128]{3,2,1,0:T(8,128)S(1)} %copy-done.5), kind=kOutput, calls=%fused_computation.12 | convolution fusion | flops 806354944 | bytes 8454145 | tf_op jit(solution)/shard_map/dot_general | solution.py:50
  92.0 3.5 %fusion.48 = f32[128,128]{1,0:T(8,128)S(1)} fusion(f32[4096,128]{1,0:T(8,128)S(1)} %convolution_add_fusion.1), kind=kOutput, calls=%fused_computation.68 | convolution fusion | flops 805306368 | bytes 2162688 | tf_op jit(solution)/shard_map/...pk,...pl->...kl/dot_general | solution.py:31
  95.4 31.4 %all-gather.1 = f32[1024,128]{1,0:T(8,128)S(1)} all-gather(f32[128,128]{1,0:T(8,128)S(1)} %fusion.48), channel_id=3, replica_groups=mesh['coord'=8,'cohort'=4] {'coord'}, dimensions={0}, use_global_device_ids=true | all-gather | bytes 589824 | tf_op jit(solution)/shard_map/all_gather | solution.py:11
  127.0 11.7 %cholesky.70 = f32[128,128]{1,0:T(8,128)S(1)} custom-call(f32[128,128]{1,0:T(8,128)S(1)} %fusion.37), custom_call_target="Cholesky" | custom-call | tf_op jit(solution)/shard_map/jit(cholesky)/cholesky | solution.py:20
  140.0 9.8 %custom-call.8 = f32[1,128,128]{1,2,0:T(8,128)S(1)} custom-call(f32[1,128,128]{2,1,0:T(8,128)S(1)} %fusion.30), custom_call_target="InvertDiagBlocksLowerTriangular" | custom-call | tf_op jit(solution)/shard_map/jit(_solve_triangular)/triangular_solve | solution.py:22
  150.1 3.1 fusion.49
  154.7 38.9 %collective-permute-done.1 = f32[4096,128]{1,0:T(8,128)S(1)} collective-permute-done((f32[4096,128]{1,0:T(8,128)}, f32[4096,128]{1,0:T(8,128)S(1)}, u32[]{:S(2)}, u32[]{:S(2)}) %collective-permute-start.1) | collective-permute-done | bytes 2097184 | tf_op jit(solution)/shard_map/ppermute | solution.py:16
  196.9 3.5 %convolution_add_fusion = f32[4096,128]{1,0:T(8,128)S(1)} fusion(f32[4096,128]{1,0:T(8,128)S(1)} %fusion.10, f32[4096,128]{1,0:T(8,128)} %copy-done.3, f32[4096,128]{1,0:T(8,128)} %fusion.49, pred[]{:T(512)S(6)} %eq.15, f32[2,2,128,128]{3,2,1,0:T(8,128)S(1)} %copy-done.5), kind=kOutput, calls=%fused_computation.11 | convolution fusion | flops 806354944 | bytes 8454145 | tf_op jit(solution)/shard_map/dot_general | solution.py:50
  200.3 3.5 %fusion.50 = f32[128,128]{1,0:T(8,128)S(1)} fusion(f32[4096,128]{1,0:T(8,128)S(1)} %convolution_add_fusion), kind=kOutput, calls=%fused_computation.70 | convolution fusion | flops 805306368 | bytes 2162688 | tf_op jit(solution)/shard_map/...pk,...pl->...kl/dot_general | solution.py:31
  203.8 31.2 %all-gather.2 = f32[1024,128]{1,0:T(8,128)S(1)} all-gather(f32[128,128]{1,0:T(8,128)S(1)} %fusion.50), channel_id=4, replica_groups=mesh['coord'=8,'cohort'=4] {'coord'}, dimensions={0}, use_global_device_ids=true | all-gather | bytes 589824 | tf_op jit(solution)/shard_map/all_gather | solution.py:11
  235.2 11.7 %cholesky.81 = f32[128,128]{1,0:T(8,128)S(1)} custom-call(f32[128,128]{1,0:T(8,128)S(1)} %fusion.33), custom_call_target="Cholesky" | custom-call | tf_op jit(solution)/shard_map/jit(cholesky)/cholesky | solution.py:20
  248.2 9.8 %custom-call.9 = f32[1,128,128]{1,2,0:T(8,128)S(1)} custom-call(f32[1,128,128]{2,1,0:T(8,128)S(1)} %fusion.31), custom_call_target="InvertDiagBlocksLowerTriangular" | custom-call | tf_op jit(solution)/shard_map/jit(_solve_triangular)/triangular_solve | solution.py:22
  261.6 6.5 %fusion.3 = f32[1024,128]{1,0:T(8,128)} fusion(bf16[1,1024,4096]{2,1,0:T(8,128)(2,1)} %param.6, f32[4096]{0:T(1024)S(1)} %broadcast_multiply_fusion, f32[4096,128]{1,0:T(8,128)S(1)} %fusion.51), kind=kOutput, calls=%fused_computation.6 | convolution fusion | flops 1086849024 | bytes 11026432 | tf_op jit(solution)/shard_map/dot_general | solution.py:59
  268.1 3.1 multiply_bitcast_fusion
  271.2 63.0 %reduce-scatter.2.cloned.1.call-done = f32[128,128]{1,0:T(8,128)} async-done(((f32[1024,128]{1,0:T(8,128)}), f32[128,128]{1,0:T(8,128)}) %reduce-scatter.2.cloned.1.call-update) | async-done | bytes 65552 | tf_op jit(solution)/shard_map/reduce_scatter | solution.py:58
  (41 shorter events, 15.8 us)
Async XLA Ops:
  7.2 327.1 %reduce-scatter.2.cloned.1.call-start = ((), (), s32[]{:S(2)}) async-start(), calls=%async_computation.1 | async-start | bytes 589824 | tf_op jit(solution)/shard_map/reduce_scatter | solution.py:58
  7.2 5.8 %copy-start.2 = (bf16[1,1024,4096]{2,1,0:T(8,128)(2,1)S(1)}, bf16[1,1024,4096]{2,1,0:T(8,128)(2,1)}, u32[]{:S(2)}) copy-start(bf16[1,1024,4096]{2,1,0:T(8,128)(2,1)} %param.6) | copy-start | bytes 25165828
  16.8 3.6 %copy-start.1 = (f32[4096,128]{1,0:T(8,128)}, f32[4096,128]{1,0:T(8,128)S(1)}, u32[]{:S(2)}) copy-start(f32[4096,128]{1,0:T(8,128)S(1)} %fusion.6) | copy-start | bytes 6291460
  77.2 7.8 %copy-start.5 = (f32[2,2,128,128]{3,2,1,0:T(8,128)S(1)}, f32[2,2,128,128]{3,2,1,0:T(8,128)}, u32[]{:S(2)}) copy-start(f32[2,2,128,128]{3,2,1,0:T(8,128)} %param.8) | copy-start | bytes 786436
  80.7 4.4 %copy-start = (f32[4096,128]{1,0:T(8,128)}, f32[4096,128]{1,0:T(8,128)S(1)}, u32[]{:S(2)}) copy-start(f32[4096,128]{1,0:T(8,128)S(1)} %fusion.47) | copy-start | bytes 6291460
  80.7 4.4 %collective-permute-start = (f32[4096,128]{1,0:T(8,128)S(1)}, f32[4096,128]{1,0:T(8,128)}, u32[]{:S(2)}, u32[]{:S(2)}) collective-permute-start(f32[4096,128]{1,0:T(8,128)S(1)} %fusion.47), channel_id=1, source_target_pairs={{0,1},{1,0},{2,3},{3,2},{4,5},{5,4},{6,7},{7,6},{8,9},{9,8},{10,11... | collective-permute-start | bytes 6291464 | tf_op jit(solution)/shard_map/ppermute | solution.py:16
  153.2 40.4 %collective-permute-start.1 = (f32[4096,128]{1,0:T(8,128)}, f32[4096,128]{1,0:T(8,128)S(1)}, u32[]{:S(2)}, u32[]{:S(2)}) collective-permute-start(f32[4096,128]{1,0:T(8,128)} %fusion.49), channel_id=1, source_target_pairs={{0,2},{1,3},{2,0},{3,1},{4,6},{5,7},{6,4},{7,5},{8,10},{9,11},{10,... | collective-permute-start | bytes 6291464 | tf_op jit(solution)/shard_map/ppermute | solution.py:16
  193.6 1.4 copy-start.3
  260.2 1.3 copy-start.4
Sparse Core Ops, SparseCore 0:
  268.2 65.9 reduce-scatter.1
